TPU v7x, 256 devices: a whole 4x4x8 slice. The times are simulated.
256 devices in a mesh: dom: 64 (over y, z, core), rep: 4 (over x).
Axes of the slice: x: 4, y: 4, z: 8, core: 2. Of those that a mesh axis runs over, the one named last changes fastest.
Arguments:
- feats: bfloat16 [256, 262144], P('rep', 'dom'), may hold values from -6 to 6
- w_self: bfloat16 [256, 256], P(None, 'rep'), may hold values from -0.375 to 0.375
- w_neigh: bfloat16 [256, 256], P(None, 'rep'), may hold values from -3 to 3
- local_cols: int32 [2048, 2], P('dom'), may hold values from 0 to 31
- local_tiles: bfloat16 [2048, 2, 128, 128], P('dom'), may hold values from 0 to 3, as said below
- send_list: int32 [64, 64, 2], P('dom'), may hold values from 0 to 31
- remote_rows: int32 [64, 64, 2], P('dom'), may hold values from 0 to 31
- remote_tiles: bfloat16 [64, 64, 2, 128, 128], P('dom'), may hold values from 0 to 3, as said below
- cotangent: bfloat16 [256, 262144], P('rep', 'dom'), may hold values from -6 to 6
Outputs:
- output: bfloat16 [256, 262144], P('rep', 'dom')
- grad_feats: bfloat16 [256, 262144], P('rep', 'dom')
- grad_w_self: float32 [256, 256], P(None, 'rep')
- grad_w_neigh: float32 [256, 256], P(None, 'rep')
Inputs may be any that keep to these rules, and one draw needn't show every extreme that they name: `local_tiles`: edge weights: zero where a tile has no edge, positive otherwise. `remote_tiles`: edge weights: zero where a tile has no edge, positive otherwise.
All inputs are finite; a program needn't handle non-finite values.
Results may differ from a plain program's by a relative error of at most 0.0055.
Values may be sent and summed in bfloat16 or wider, within the bound.
No kernel may reach another device: no remote copies, remote signals or barrier semaphores. Data moves between devices by JAX's collectives and lax.ppermute only.
A program may use at most 128 MiB of HBM per device.

v0:
```python
import jax
import jax.numpy as jnp
from jax import lax
from jax.sharding import PartitionSpec as P


def local(
    feats, w_self, w_neigh, local_cols, local_tiles, send_list, remote_rows, remote_tiles, cotangent
):
    highest = lax.Precision.HIGHEST
    feat_width, node_count = feats.shape
    blocks, local_links, tile_side, _ = local_tiles.shape
    block_ids = jnp.arange(blocks, dtype=jnp.int32)
    blocked = feats.reshape(feat_width, blocks, tile_side)
    outgoing = blocked[:, send_list[0]]
    incoming = lax.all_to_all(outgoing, "dom", split_axis=1, concat_axis=1, tiled=True)
    full_feats = lax.all_gather(feats, "rep", axis=0, tiled=True)
    gathered = blocked[:, local_cols]
    summed = jnp.einsum("fblj,blij->fbi", gathered, local_tiles, preferred_element_type=jnp.float32)
    weight_rows = jnp.sum(local_tiles, axis=(1, 3), dtype=jnp.float32)
    far_tiles = remote_tiles[0]
    far_rows = remote_rows[0]
    placing = (far_rows[:, :, None] == block_ids).astype(jnp.float32)
    far_sums = jnp.sum(far_tiles, axis=3, dtype=jnp.float32)
    divisor = 1.0 + weight_rows + jnp.einsum("ski,skb->bi", far_sums, placing, precision=highest)
    far_terms = jnp.einsum(
        "fskj,skij->fski", incoming, far_tiles, preferred_element_type=jnp.float32
    )
    summed = summed + jnp.einsum("fski,skb->fbi", far_terms, placing, precision=highest)
    aggregate = (summed / divisor).astype(jnp.bfloat16).reshape(feat_width, node_count)
    full_agg = lax.all_gather(aggregate, "rep", axis=0, tiled=True)
    preact = jnp.einsum("ab,an->bn", w_self, full_feats, preferred_element_type=jnp.float32)
    preact = preact + jnp.einsum("ab,an->bn", w_neigh, full_agg, preferred_element_type=jnp.float32)
    sigmoid_val = jax.nn.sigmoid(preact)
    output = (preact * sigmoid_val).astype(jnp.bfloat16)
    slope = sigmoid_val * (1.0 + preact * (1.0 - sigmoid_val))
    grad_pre = (cotangent.astype(jnp.float32) * slope).astype(jnp.bfloat16)
    wg_self = jnp.einsum("an,bn->ab", full_feats, grad_pre, preferred_element_type=jnp.float32)
    wg_neigh = jnp.einsum("an,bn->ab", full_agg, grad_pre, preferred_element_type=jnp.float32)
    wg_self, wg_neigh = lax.psum((wg_self, wg_neigh), "dom")
    term_self = jnp.dot(w_self, grad_pre, preferred_element_type=jnp.float32)
    term_neigh = jnp.dot(w_neigh, grad_pre, preferred_element_type=jnp.float32)
    stacked = lax.psum_scatter(
        jnp.concatenate([term_self, term_neigh], axis=1), "rep", scatter_dimension=0, tiled=True
    )
    back_self = stacked[:, :node_count]
    back_agg = stacked[:, node_count:]
    scaled = (back_agg.reshape(feat_width, blocks, tile_side) / divisor).astype(jnp.bfloat16)
    picked = scaled[:, far_rows]
    far_back = jnp.einsum("fski,skij->fskj", picked, far_tiles, preferred_element_type=jnp.float32)
    returned = lax.all_to_all(far_back, "dom", split_axis=1, concat_axis=1, tiled=True)
    near_back = jnp.einsum(
        "fbi,blij->fblj", scaled, local_tiles, preferred_element_type=jnp.float32
    )
    landing = (local_cols[:, :, None] == block_ids).astype(jnp.float32)
    collected = jnp.einsum("fblj,blc->fcj", near_back, landing, precision=highest)
    homing = (send_list[0][:, :, None] == block_ids).astype(jnp.float32)
    collected = collected + jnp.einsum("fdkj,dkc->fcj", returned, homing, precision=highest)
    grad_feats = (back_self + collected.reshape(feat_width, node_count)).astype(jnp.bfloat16)
    return (output, grad_feats, wg_self, wg_neigh)


def solution(mesh):
    placed = (
        P("rep", "dom"),
        P(None, "rep"),
        P(None, "rep"),
        P("dom", None),
        P("dom", None, None, None),
        P("dom", None, None),
        P("dom", None, None),
        P("dom", None, None, None, None),
        P("rep", "dom"),
    )
    return jax.shard_map(
        local,
        mesh=mesh,
        in_specs=placed,
        out_specs=(P("rep", "dom"), P("rep", "dom"), P(None, "rep"), P(None, "rep")),
        check_vma=False,
    )
```

profile of v0, /device:TPU:1, one launch (start us, length us, event | category | flops | bytes accessed | tf_op | source)
XLA Modules:
  0.0 480.7 jit_solution(3183939513342969295)
XLA Ops:
  9.3 2.1 gather_fusion.1
  11.5 13.3 %all-to-all-start = ((bf16[64,64,2,128]{3,0,2,1:T(8,128)(2,1)}), bf16[64,64,2,128]{3,0,2,1:T(8,128)(2,1)S(1)}, u32[]{:S(2)}, u32[]{:S(2)}) async-start(bf16[64,64,2,128]{3,0,2,1:T(8,128)(2,1)} %bitcast.123), calls=%async_computation | async-start | bytes 4194304 | tf_op jit(solution)/shard_map/all_to_all | solution.py:16
  26.7 2.2 convert_reduce_fusion.1
  28.9 3.4 convert_reduce_fusion
  32.5 43.5 %all-to-all-done = bf16[64,64,2,128]{3,0,2,1:T(8,128)(2,1)S(1)} async-done(((bf16[64,64,2,128]{3,0,2,1:T(8,128)(2,1)}), bf16[64,64,2,128]{3,0,2,1:T(8,128)(2,1)S(1)}, u32[]{:S(2)}, u32[]{:S(2)}) %all-to-all-start) | async-done | bytes 2097184 | tf_op jit(solution)/shard_map/all_to_all | solution.py:16
  76.0 5.1 %fusion.8 = f32[64,64,2,128]{3,0,2,1:T(8,128)S(1)} fusion(bf16[64,64,2,128]{3,0,2,1:T(8,128)(2,1)S(1)} %all-to-all-done, bf16[1,64,2,128,128]{4,3,2,1,0:T(8,128)(2,1)} %param.16), kind=kOutput, calls=%fused_computation.18 | convolution fusion | flops 268435456 | bytes 10485760 | tf_op jit(solution)/shard_map/fskj,skij->fski/dot_general | solution.py:26
  81.2 4.0 fusion.20
  88.2 29.0 %all-gather.5.cloned.1.call-done = bf16[256,4096]{1,0:T(8,128)(2,1)} async-done(((bf16[64,4096]{1,0:T(8,128)(2,1)}), bf16[256,4096]{1,0:T(8,128)(2,1)}) %all-gather.5.cloned.1.call-update) | async-done | bytes 2097168 | tf_op jit(solution)/shard_map/all_gather | solution.py:31
  117.2 2.1 convolution_bitcast_fusion.2
  119.2 33.2 %all-gather.3.cloned.1.call-done = bf16[256,4096]{1,0:T(8,128)(2,1)} async-done(((bf16[64,4096]{1,0:T(8,128)(2,1)}), bf16[256,4096]{1,0:T(8,128)(2,1)}) %all-gather.3.cloned.1.call-update) | async-done | bytes 2097168 | tf_op jit(solution)/shard_map/all_gather | solution.py:17
  152.4 3.2 multiply_convert_fusion
  157.1 3.8 pad_maximum_fusion
  160.9 8.9 %copy.60 = f32[256,8192]{1,0:T(8,128)} copy(f32[256,8192]{0,1:T(8,128)} %pad_maximum_fusion) | data formatting | bytes 16777216
  170.1 83.0 %reduce-scatter.4.cloned.1.call-done = f32[64,8192]{1,0:T(8,128)} async-done(((f32[256,8192]{1,0:T(8,128)}), f32[64,8192]{1,0:T(8,128)}) %reduce-scatter.4.cloned.1.call-update) | async-done | bytes 2097168
  253.1 3.1 fusion.49
  256.2 1.8 copy.63
  261.9 5.4 %fusion.11 = f32[64,64,2,128]{3,0,2,1:T(8,128)} fusion(bf16[64,64,2,128]{3,0,2,1:T(8,128)(2,1)S(1)} %bitcast.121, bf16[1,64,2,128,128]{4,3,2,1,0:T(8,128)(2,1)} %param.16), kind=kOutput, calls=%fused_computation.19 | convolution fusion | flops 268435456 | bytes 10485760 | tf_op jit(solution)/shard_map/fski,skij->fskj/dot_general | solution.py:50
  267.3 11.0 %all-to-all-start.1 = ((f32[64,64,2,128]{3,0,2,1:T(8,128)}), f32[64,64,2,128]{3,0,2,1:T(8,128)}, u32[]{:S(2)}, u32[]{:S(2)}) async-start(f32[64,64,2,128]{3,0,2,1:T(8,128)} %fusion.11), calls=%async_computation.1 | async-start | bytes 8388608 | tf_op jit(solution)/shard_map/all_to_all | solution.py:51
  281.6 3.4 copy.62
  285.4 2.1 fusion.17
  287.5 87.6 %all-to-all-done.1 = f32[64,64,2,128]{3,0,2,1:T(8,128)} async-done(((f32[64,64,2,128]{3,0,2,1:T(8,128)}), f32[64,64,2,128]{3,0,2,1:T(8,128)}, u32[]{:S(2)}, u32[]{:S(2)}) %all-to-all-start.1) | async-done | bytes 4194336 | tf_op jit(solution)/shard_map/all_to_all | solution.py:51
  375.1 5.9 %fusion.31 = f32[64,32,128]{2,1,0:T(8,128)S(1)} fusion(f32[32,64,128]{2,0,1:T(8,128)S(1)} %fusion.17, f32[64,64,2,128]{3,0,2,1:T(8,128)} %all-to-all-done.1, s32[64,2]{0,1:T(2,128)S(1)} %bitcast.128), kind=kOutput, calls=%fused_computation.32 | convolution fusion | flops 402919424 | bytes 6291968 | tf_op jit(solution)/shard_map/fdkj,dkc->fcj/dot_general | solution.py:58
  381.0 2.0 copy.59
  386.0 85.2 %all-reduce.3.cloned.1.call-done = (f32[256,64]{0,1:T(8,128)}, f32[256,64]{0,1:T(8,128)}) async-done(((f32[256,64]{0,1:T(8,128)}, f32[256,64]{0,1:T(8,128)}), (f32[256,64]{0,1:T(8,128)}, f32[256,64]{0,1:T(8,128)})) %all-reduce.3.cloned.1.call-update) | async-done | bytes 131088 | tf_op jit(solution)/shard_map/psum | solution.py:40
  (63 shorter events, 22.4 us)
Async XLA Ops:
  7.2 145.3 %copy-start = (bf16[256,64]{0,1:T(8,128)(2,1)S(1)}, bf16[256,64]{0,1:T(8,128)(2,1)}, u32[]{:S(2)}) copy-start(bf16[256,64]{0,1:T(8,128)(2,1)} %param.10) | copy-start | bytes 98308
  11.5 13.3 %copy-start.10 = (s32[32,2]{0,1:T(2,128)S(1)}, s32[32,2]{0,1:T(2,128)}, u32[]{:S(2)}) copy-start(s32[32,2]{0,1:T(2,128)} %param.12) | copy-start | bytes 772
  11.5 64.5 %all-to-all-start = ((bf16[64,64,2,128]{3,0,2,1:T(8,128)(2,1)}), bf16[64,64,2,128]{3,0,2,1:T(8,128)(2,1)S(1)}, u32[]{:S(2)}, u32[]{:S(2)}) async-start(bf16[64,64,2,128]{3,0,2,1:T(8,128)(2,1)} %bitcast.123), calls=%async_computation | async-start | bytes 4194304 | tf_op jit(solution)/shard_map/all_to_all | solution.py:16
  24.8 92.4 %all-gather.5.cloned.1.call-start = ((), (), s32[]{:S(2)}) async-start(), calls=%async_computation.4 | async-start | bytes 2621440 | tf_op jit(solution)/shard_map/all_gather | solution.py:31
  28.9 3.4 copy-start.9
  81.1 4.0 copy-start.2
  81.1 4.0 copy-start.7
  86.3 30.9 %copy-start.8 = (bf16[256,64]{0,1:T(8,128)(2,1)S(1)}, bf16[256,64]{0,1:T(8,128)(2,1)}, u32[]{:S(2)}) copy-start(bf16[256,64]{0,1:T(8,128)(2,1)} %param.11) | copy-start | bytes 98308
  87.2 65.3 %copy-start.12 = (bf16[64,4096]{1,0:T(8,128)(2,1)S(1)}, bf16[64,4096]{1,0:T(8,128)(2,1)}, u32[]{:S(2)}) copy-start(bf16[64,4096]{1,0:T(8,128)(2,1)} %param.17) | copy-start | bytes 1572868
  87.2 65.3 %all-gather.3.cloned.1.call-start = ((), (), s32[]{:S(2)}) async-start(), calls=%async_computation.3 | async-start | bytes 2621440 | tf_op jit(solution)/shard_map/all_gather | solution.py:17
  87.9 165.2 %reduce-scatter.4.cloned.1.call-start = ((), (), s32[]{:S(2)}) async-start(), calls=%async_computation.5 | async-start | bytes 10485760
  267.3 11.2 %copy-start.4 = (bf16[256,4096]{1,0:T(8,128)(2,1)S(1)}, bf16[256,4096]{1,0:T(8,128)(2,1)}, u32[]{:S(2)}) copy-start(bf16[256,4096]{1,0:T(8,128)(2,1)} %all-gather.5.cloned.1.call-done) | copy-start | bytes 6291460
  267.3 107.7 %all-to-all-start.1 = ((f32[64,64,2,128]{3,0,2,1:T(8,128)}), f32[64,64,2,128]{3,0,2,1:T(8,128)}, u32[]{:S(2)}, u32[]{:S(2)}) async-start(f32[64,64,2,128]{3,0,2,1:T(8,128)} %fusion.11), calls=%async_computation.1 | async-start | bytes 8388608 | tf_op jit(solution)/shard_map/all_to_all | solution.py:51
  278.3 192.9 %all-reduce.3.cloned.1.call-start = ((), (), s32[]{:S(2)}) async-start(), calls=%async_computation.6 | async-start | bytes 262144 | tf_op jit(solution)/shard_map/psum | solution.py:40
  278.6 1.6 copy-start.6
  281.6 3.4 copy-start.3
  285.4 89.6 %copy-start.11 = (s32[1,64,2]{1,2,0:T(2,128)S(1)}, s32[1,64,2]{1,2,0:T(2,128)}, u32[]{:S(2)}) copy-start(s32[1,64,2]{1,2,0:T(2,128)} %param.14) | copy-start | bytes 1540
  381.0 2.0 copy-start.5
  383.0 91.1 %copy-start.1 = (bf16[256,64]{0,1:T(8,128)(2,1)S(1)}, bf16[256,64]{0,1:T(8,128)(2,1)}, u32[]{:S(2)}) copy-start(bf16[256,64]{0,1:T(8,128)(2,1)} %param.10) | copy-start | bytes 98308
Sparse Core Ops, SparseCore 0:
  87.3 29.8 all-gather.4
  119.0 33.4 all-gather.2
  169.9 83.1 reduce-scatter.3
  283.0 188.1 all-reduce.2
where the time goes:
time: 482 us; the launch traced here: 481 us
  waiting for transfers between devices  362 us (75%)
  matrix products  33.7 us (7%)
  local copies, waits for them, and re-layouts  32.6 us (7%)
  starting transfers between devices  24.8 us (5%)
  between operations  14 us (3%)
  other arithmetic  13.2 us (3%)
    all_to_all x1, waiting for transfers between devices, local(): lax.all_to_all(far_back, 'dom', split_axis=1, concat_axis=1, tiled=True)  87.6 us
    psum x1, waiting for transfers between devices, local(): wg_self, wg_neigh = lax.psum((wg_self, wg_neigh), 'dom')  85.2 us
    unnamed x5, waiting for transfers between devices  83.8 us
    all_to_all x1, waiting for transfers between devices, local(): lax.all_to_all(outgoing, 'dom', split_axis=1, concat_axis=1, tiled=True)  43.5 us
    all_gather x1, waiting for transfers between devices, local(): full_feats = lax.all_gather(feats, 'rep', axis=0, tiled=True)  33.2 us
    all_gather x1, waiting for transfers between devices, local(): full_agg = lax.all_gather(aggregate, 'rep', axis=0, tiled=True)  29 us
    unnamed x32, local copies, waits for them, and re-layouts  18.5 us
    all_to_all x1, starting transfers between devices, local(): lax.all_to_all(outgoing, 'dom', split_axis=1, concat_axis=1, tiled=True)  13.3 us
  transfers between devices with their start and end apart: 6, of which 6 were waited for; matrix products, arithmetic and copies ran while one was open for 6% of the time, Pallas kernels for 0%

commit v1 on v0

--- a/solution.py
+++ b/solution.py
@@ -2,6 +2,12 @@
 import jax.numpy as jnp
 from jax import lax
 from jax.sharding import PartitionSpec as P
+
+
+def joined_along(blocks, dim):
+    lengths = list(blocks.shape[1:])
+    lengths[dim] *= blocks.shape[0]
+    return jnp.moveaxis(blocks, 0, dim).reshape(lengths)
 
 
 def local(
@@ -28,7 +34,19 @@
     )
     summed = summed + jnp.einsum("fski,skb->fbi", far_terms, placing, precision=highest)
     aggregate = (summed / divisor).astype(jnp.bfloat16).reshape(feat_width, node_count)
-    full_agg = lax.all_gather(aggregate, "rep", axis=0, tiled=True)
+    size = lax.axis_size("rep")
+    pairs = [(i, (i + 1) % size) for i in range(size)]
+    back = [(b, a) for a, b in pairs]
+    lower, upper = ([], [])
+    for step in range(size - 1):
+        if step % 2 == 0:
+            lower.append(lax.ppermute(lower[-1] if lower else aggregate, "rep", pairs))
+        else:
+            upper.append(lax.ppermute(upper[-1] if upper else aggregate, "rep", back))
+    tiles = jnp.stack([*lower[::-1], aggregate, *upper])
+    shift = lax.axis_index("rep") - len(lower)
+    tiles = tiles[(jnp.arange(size) - shift) % size]
+    full_agg = joined_along(tiles, 0)
     preact = jnp.einsum("ab,an->bn", w_self, full_feats, preferred_element_type=jnp.float32)
     preact = preact + jnp.einsum("ab,an->bn", w_neigh, full_agg, preferred_element_type=jnp.float32)
     sigmoid_val = jax.nn.sigmoid(preact)

time: 482 us -> 450 us (0.934)
  waiting for transfers between devices: 362 us -> 319 us
  local copies, waits for them, and re-layouts: 32.6 us -> 38.9 us
    all_gather x1, waiting for transfers between devices: 33.2 us -> 0.01 us  [local(): full_feats = lax.all_gather(feats, 'rep', axis=0, tiled=True)]
    all_gather x1 -> x0, waiting for transfers between devices: 29 us -> none  [local(): full_agg = lax.all_gather(aggregate, 'rep', axis=0, tiled=True)]
    ppermute x0 -> x3, waiting for transfers between devices: none -> 24.4 us  [the longest x2 24.4 us: local(): lower.append(lax.ppermute(lower[-1] if lower else aggregate, 'rep', pairs))]
    unnamed x5 -> x4, waiting for transfers between devices: 83.8 us -> 80.1 us
    unnamed x32 -> x28, local copies, waits for them, and re-layouts: 18.5 us -> 19.8 us
  transfers between devices with their start and end apart: 6 -> 8, of which waited for: 6 -> 6; matrix products, arithmetic and copies ran while one was open for 6% -> 10% of each run, Pallas kernels for 0% -> 0%
where the time goes in v1:
time: 450 us; the launch traced here: 448 us
  waiting for transfers between devices  319 us (71%)
  local copies, waits for them, and re-layouts  38.9 us (9%)
  matrix products  34.1 us (8%)
  starting transfers between devices  27.2 us (6%)
  other arithmetic  14.9 us (3%)
  between operations  14 us (3%)
    all_to_all x1, waiting for transfers between devices, local(): lax.all_to_all(far_back, 'dom', split_axis=1, concat_axis=1, tiled=True)  87.6 us
    psum x1, waiting for transfers between devices, local(): wg_self, wg_neigh = lax.psum((wg_self, wg_neigh), 'dom')  84.5 us
    unnamed x4, waiting for transfers between devices  80.1 us
    all_to_all x1, waiting for transfers between devices, local(): lax.all_to_all(outgoing, 'dom', split_axis=1, concat_axis=1, tiled=True)  42.8 us
    ppermute x2, waiting for transfers between devices, local(): lower.append(lax.ppermute(lower[-1] if lower else aggregate, 'rep', pairs))  24.4 us
    unnamed x28, local copies, waits for them, and re-layouts  19.8 us
    all_to_all x1, starting transfers between devices, local(): lax.all_to_all(outgoing, 'dom', split_axis=1, concat_axis=1, tiled=True)  13.3 us
    all_to_all x1, starting transfers between devices, local(): lax.all_to_all(far_back, 'dom', split_axis=1, concat_axis=1, tiled=True)  10.8 us
  transfers between devices with their start and end apart: 8, of which 6 were waited for; matrix products, arithmetic and copies ran while one was open for 10% of the time, Pallas kernels for 0%

profile of v1, /device:TPU:1, one launch (start us, length us, event | category | flops | bytes accessed | tf_op | source)
XLA Modules:
  0.0 448.5 jit_solution(6771190184848384021)
XLA Ops:
  9.3 2.2 gather_fusion.1
  11.5 13.3 %all-to-all-start = ((bf16[64,64,2,128]{3,0,2,1:T(8,128)(2,1)}), bf16[64,64,2,128]{3,0,2,1:T(8,128)(2,1)S(1)}, u32[]{:S(2)}, u32[]{:S(2)}) async-start(bf16[64,64,2,128]{3,0,2,1:T(8,128)(2,1)} %bitcast.129), calls=%async_computation | async-start | bytes 4194304 | tf_op jit(solution)/shard_map/all_to_all | solution.py:22
  27.4 2.2 convert_reduce_fusion.1
  29.6 3.4 convert_reduce_fusion
  33.3 42.8 %all-to-all-done = bf16[64,64,2,128]{3,0,2,1:T(8,128)(2,1)S(1)} async-done(((bf16[64,64,2,128]{3,0,2,1:T(8,128)(2,1)}), bf16[64,64,2,128]{3,0,2,1:T(8,128)(2,1)S(1)}, u32[]{:S(2)}, u32[]{:S(2)}) %all-to-all-start) | async-done | bytes 2097184 | tf_op jit(solution)/shard_map/all_to_all | solution.py:22
  76.0 5.2 %fusion.8 = f32[64,64,2,128]{3,0,2,1:T(8,128)S(1)} fusion(bf16[64,64,2,128]{3,0,2,1:T(8,128)(2,1)S(1)} %all-to-all-done, bf16[1,64,2,128,128]{4,3,2,1,0:T(8,128)(2,1)} %param.16), kind=kOutput, calls=%fused_computation.19 | convolution fusion | flops 268435456 | bytes 10485760 | tf_op jit(solution)/shard_map/fskj,skij->fski/dot_general | solution.py:32
  81.2 4.0 fusion.20
  89.1 11.6 %collective-permute-done = bf16[64,4096]{1,0:T(8,128)(2,1)S(1)} collective-permute-done((bf16[64,4096]{1,0:T(8,128)(2,1)S(1)}, bf16[64,4096]{1,0:T(8,128)(2,1)S(1)}, u32[]{:S(2)}, u32[]{:S(2)}) %collective-permute-start) | collective-permute-done | bytes 524320 | tf_op jit(solution)/shard_map/ppermute | solution.py:43
  101.4 12.8 %collective-permute-done.1 = bf16[64,4096]{1,0:T(8,128)(2,1)S(1)} collective-permute-done((bf16[64,4096]{1,0:T(8,128)(2,1)S(1)}, bf16[64,4096]{1,0:T(8,128)(2,1)S(1)}, u32[]{:S(2)}, u32[]{:S(2)}) %collective-permute-start.1) | collective-permute-done | bytes 524320 | tf_op jit(solution)/shard_map/ppermute | solution.py:43
  115.7 2.3 gather_fusion.2
  119.5 3.6 multiply_convert_fusion
  124.6 3.8 pad_maximum_fusion
  128.4 9.0 %copy.63 = f32[256,8192]{1,0:T(8,128)} copy(f32[256,8192]{0,1:T(8,128)} %pad_maximum_fusion) | data formatting | bytes 16777216
  137.6 79.4 %reduce-scatter.4.cloned.1.call-done = f32[64,8192]{1,0:T(8,128)} async-done(((f32[256,8192]{1,0:T(8,128)}), f32[64,8192]{1,0:T(8,128)}) %reduce-scatter.4.cloned.1.call-update) | async-done | bytes 2097168
  217.0 3.1 fusion.50
  220.1 3.2 copy.66
  223.3 3.2 copy.51
  227.8 2.2 gather_fusion.3
  230.0 6.0 %fusion.11 = f32[64,64,2,128]{3,0,2,1:T(8,128)} fusion(bf16[64,64,2,128]{3,0,2,1:T(8,128)(2,1)} %bitcast.127, bf16[1,64,2,128,128]{4,3,2,1,0:T(8,128)(2,1)} %param.16), kind=kOutput, calls=%fused_computation.20 | convolution fusion | flops 268435456 | bytes 10485760 | tf_op jit(solution)/shard_map/fski,skij->fskj/dot_general | solution.py:68
  236.0 10.8 %all-to-all-start.1 = ((f32[64,64,2,128]{3,0,2,1:T(8,128)}), f32[64,64,2,128]{3,0,2,1:T(8,128)}, u32[]{:S(2)}, u32[]{:S(2)}) async-start(f32[64,64,2,128]{3,0,2,1:T(8,128)} %fusion.11), calls=%async_computation.1 | async-start | bytes 8388608 | tf_op jit(solution)/shard_map/all_to_all | solution.py:69
  250.1 3.4 copy.65
  256.0 87.6 %all-to-all-done.1 = f32[64,64,2,128]{3,0,2,1:T(8,128)} async-done(((f32[64,64,2,128]{3,0,2,1:T(8,128)}), f32[64,64,2,128]{3,0,2,1:T(8,128)}, u32[]{:S(2)}, u32[]{:S(2)}) %all-to-all-start.1) | async-done | bytes 4194336 | tf_op jit(solution)/shard_map/all_to_all | solution.py:69
  343.6 5.9 %fusion.31 = f32[64,32,128]{2,1,0:T(8,128)S(1)} fusion(f32[32,64,128]{2,0,1:T(8,128)S(1)} %fusion.17, f32[64,64,2,128]{3,0,2,1:T(8,128)} %all-to-all-done.1, s32[64,2]{0,1:T(2,128)S(1)} %bitcast.137), kind=kOutput, calls=%fused_computation.34 | convolution fusion | flops 402919424 | bytes 6291968 | tf_op jit(solution)/shard_map/fdkj,dkc->fcj/dot_general | solution.py:76
  354.5 84.5 %all-reduce.3.cloned.1.call-done = (f32[256,64]{0,1:T(8,128)}, f32[256,64]{0,1:T(8,128)}) async-done(((f32[256,64]{0,1:T(8,128)}, f32[256,64]{0,1:T(8,128)}), (f32[256,64]{0,1:T(8,128)}, f32[256,64]{0,1:T(8,128)})) %all-reduce.3.cloned.1.call-update) | async-done | bytes 131088 | tf_op jit(solution)/shard_map/psum | solution.py:58
  (68 shorter events, 29.3 us)
Async XLA Ops:
  7.2 112.3 %copy-start = (bf16[256,64]{0,1:T(8,128)(2,1)S(1)}, bf16[256,64]{0,1:T(8,128)(2,1)}, u32[]{:S(2)}) copy-start(bf16[256,64]{0,1:T(8,128)(2,1)} %param.10) | copy-start | bytes 98308
  11.5 14.1 %copy-start.9 = (s32[32,2]{0,1:T(2,128)S(1)}, s32[32,2]{0,1:T(2,128)}, u32[]{:S(2)}) copy-start(s32[32,2]{0,1:T(2,128)} %param.12) | copy-start | bytes 772
  11.5 64.5 %all-to-all-start = ((bf16[64,64,2,128]{3,0,2,1:T(8,128)(2,1)}), bf16[64,64,2,128]{3,0,2,1:T(8,128)(2,1)S(1)}, u32[]{:S(2)}, u32[]{:S(2)}) async-start(bf16[64,64,2,128]{3,0,2,1:T(8,128)(2,1)} %bitcast.129), calls=%async_computation | async-start | bytes 4194304 | tf_op jit(solution)/shard_map/all_to_all | solution.py:22
  24.8 94.7 %all-gather.2.cloned.1.call-start = ((), (), s32[]{:S(2)}) async-start(), calls=%async_computation.3 | async-start | bytes 2621440 | tf_op jit(solution)/shard_map/all_gather | solution.py:23
  25.5 191.5 %reduce-scatter.4.cloned.1.call-start = ((), (), s32[]{:S(2)}) async-start(), calls=%async_computation.4 | async-start | bytes 10485760
  29.6 3.4 copy-start.8
  81.2 4.0 copy-start.2
  81.2 4.0 copy-start.6
  86.3 14.4 %collective-permute-start = (bf16[64,4096]{1,0:T(8,128)(2,1)S(1)}, bf16[64,4096]{1,0:T(8,128)(2,1)S(1)}, u32[]{:S(2)}, u32[]{:S(2)}) collective-permute-start(bf16[64,4096]{1,0:T(8,128)(2,1)S(1)} %copy_bitcast_fusion), channel_id=1, source_target_pairs={{0,1},{1,2},{2,3},{3,0},{4,5},{5,6},{6,7},{7,4},{8,9},{9,10},{10,1... | collective-permute-start | bytes 1572872 | tf_op jit(solution)/shard_map/ppermute | solution.py:43
  87.6 13.7 %collective-permute-start.2 = (bf16[64,4096]{1,0:T(8,128)(2,1)S(1)}, bf16[64,4096]{1,0:T(8,128)(2,1)S(1)}, u32[]{:S(2)}, u32[]{:S(2)}) collective-permute-start(bf16[64,4096]{1,0:T(8,128)(2,1)S(1)} %copy_bitcast_fusion), channel_id=1, source_target_pairs={{1,0},{2,1},{3,2},{0,3},{5,4},{6,5},{7,6},{4,7},{9,8},{10,9},{11,1... | collective-permute-start | bytes 1572872 | tf_op jit(solution)/shard_map/ppermute | solution.py:45
  100.7 13.4 %collective-permute-start.1 = (bf16[64,4096]{1,0:T(8,128)(2,1)S(1)}, bf16[64,4096]{1,0:T(8,128)(2,1)S(1)}, u32[]{:S(2)}, u32[]{:S(2)}) collective-permute-start(bf16[64,4096]{1,0:T(8,128)(2,1)S(1)} %collective-permute-done), channel_id=1, source_target_pairs={{0,1},{1,2},{2,3},{3,0},{4,5},{5,6},{6,7},{7,4},{8,9},{9,10},{10,1... | collective-permute-start | bytes 1572872 | tf_op jit(solution)/shard_map/ppermute | solution.py:43
  115.7 2.3 copy-start.7
  236.0 107.6 %all-to-all-start.1 = ((f32[64,64,2,128]{3,0,2,1:T(8,128)}), f32[64,64,2,128]{3,0,2,1:T(8,128)}, u32[]{:S(2)}, u32[]{:S(2)}) async-start(f32[64,64,2,128]{3,0,2,1:T(8,128)} %fusion.11), calls=%async_computation.1 | async-start | bytes 8388608 | tf_op jit(solution)/shard_map/all_to_all | solution.py:69
  246.8 192.2 %all-reduce.3.cloned.1.call-start = ((), (), s32[]{:S(2)}) async-start(), calls=%async_computation.5 | async-start | bytes 262144 | tf_op jit(solution)/shard_map/psum | solution.py:58
  247.1 1.6 copy-start.5
  250.1 3.4 copy-start.3
  253.9 89.7 %copy-start.10 = (s32[1,64,2]{1,2,0:T(2,128)S(1)}, s32[1,64,2]{1,2,0:T(2,128)}, u32[]{:S(2)}) copy-start(s32[1,64,2]{1,2,0:T(2,128)} %param.14) | copy-start | bytes 1540
  349.5 2.1 copy-start.4
  351.6 90.4 %copy-start.1 = (bf16[256,64]{0,1:T(8,128)(2,1)S(1)}, bf16[256,64]{0,1:T(8,128)(2,1)}, u32[]{:S(2)}) copy-start(bf16[256,64]{0,1:T(8,128)(2,1)} %param.10) | copy-start | bytes 98308
Sparse Core Ops, SparseCore 0:
  27.4 34.3 all-gather.1
  137.5 79.4 reduce-scatter.3
  251.8 187.1 all-reduce.2
